TPU v7x, 256 devices: a whole 4x4x8 slice. The times are simulated.
256 devices in a mesh: wide: 128 (over x, y, z_lo, core), head: 2 (over z_hi).
Axes of the slice: x: 4, y: 4, z: 8 (z_hi: 2, z_lo: 4; z = z_hi * 4 + z_lo), core: 2. Of those that a mesh axis runs over, the one named last changes fastest.
Arguments:
- branch_query: bfloat16 [512, 8192], P('wide', 'head'), may hold values from -6 to 6
- key_new: bfloat16 [512, 1024], P('wide', 'head'), may hold values from -6 to 6
- value_new: bfloat16 [512, 1024], P('wide', 'head'), may hold values from -6 to 6
- pool_pages: bfloat16 [2, 8192, 16, 1024], P(None, 'wide', None, 'head'), may hold values from -6 to 6
- page_table: int32 [512, 16], P('wide'), may hold values from 0 to 63, as said below
- tail_length: int32 [512], P('wide'), may hold values from 1 to 256
- parent_row: int32 [512], P('wide'), may hold values from 0 to 511, as said below
- residual: bfloat16 [512, 8192], P(('wide', 'head')), may hold values from -6 to 6
- norm_gain: float32 [8192], replicated, may hold values from 0.5 to 1.5
- gate_blocks: bfloat16 [128, 32, 128, 128], P('wide'), may hold values from -0.09375 to 0.09375
- up_blocks: bfloat16 [128, 32, 128, 128], P('wide'), may hold values from -0.09375 to 0.09375
- gate_up_keep: int32 [128, 32], P('wide'), may hold values from 0 to 63, as said below
- gate_scale: float32 [128, 32], P('wide'), may hold values from 0.5 to 2
- up_scale: float32 [128, 32], P('wide'), may hold values from 0.5 to 2
- down_blocks: bfloat16 [128, 32, 128, 128], P('wide'), may hold values from -0.0625 to 0.0625
- down_keep: int32 [128, 32], P('wide'), may hold values from 0 to 63, as said below
- down_scale: float32 [128, 32], P('wide'), may hold values from 0.5 to 2
Outputs:
- layer_out: bfloat16 [512, 8192], P(('wide', 'head'))
Inputs may be any that keep to these rules, and one draw needn't show every extreme that they name: parent_row never falls with the branch index, and parent_row[b] <= b and parent_row[b] > b - 4. `page_table`: the entries of the 4 rows held by one index of wide name each of that index's 64 pages once. `gate_up_keep`: each row names 32 different blocks. `down_keep`: each row names 32 different blocks.
All inputs are finite; a program needn't handle non-finite values.
Results may differ from a plain program's by a relative error of at most 0.017.
Values may be sent and summed in bfloat16 or wider, within the bound.
A program may use at most 64 MiB of HBM per device.

v0:
```python
import math
import jax
import jax.numpy as jnp
from jax import lax
from jax.sharding import PartitionSpec as P

HD = 128
BLK = 128


def shifted(block, axis, distance):
    devices = range(lax.axis_size(axis))
    route = [(i - distance, i) for i in devices if i - distance in devices]
    return lax.ppermute(block, axis, route)


def attend(branch_query, key_new, value_new, child_tails, child_length):
    row_count = branch_query.shape[0]
    groups = key_new.shape[1] // HD
    per_group = branch_query.shape[1] // (groups * HD)
    tail_size = child_tails.shape[2]
    queries = branch_query.reshape(row_count, groups, per_group, HD)
    tail_keys = child_tails[0].reshape(row_count, tail_size, groups, HD)
    tail_values = child_tails[1].reshape(row_count, tail_size, groups, HD)
    own_keys = key_new.reshape(row_count, groups, HD)
    own_values = value_new.reshape(row_count, groups, HD)
    factor = 1.0 / math.sqrt(HD)
    tail_scores = (
        jnp.einsum("rgjd,rtgd->rgjt", queries, tail_keys, preferred_element_type=jnp.float32)
        * factor
    )
    own_scores = (
        jnp.einsum("rgjd,rgd->rgj", queries, own_keys, preferred_element_type=jnp.float32) * factor
    )
    live_mask = (jnp.arange(tail_size, dtype=jnp.float32)[None, :] < child_length[:, None])[
        :, None, None, :
    ]
    top_score = jnp.maximum(jnp.max(jnp.where(live_mask, tail_scores, -1e30), axis=-1), own_scores)
    tail_exp = jnp.where(live_mask, jnp.exp(tail_scores - top_score[..., None]), 0.0)
    own_exp = jnp.exp(own_scores - top_score)
    totals = jnp.sum(tail_exp, axis=-1) + own_exp
    tail_weights = (tail_exp / totals[..., None]).astype(jnp.bfloat16)
    own_weights = (own_exp / totals).astype(jnp.bfloat16)
    mixture = jnp.einsum(
        "rgjt,rtgd->rgjd", tail_weights, tail_values, preferred_element_type=jnp.float32
    )
    mixture = mixture + own_weights[..., None].astype(jnp.float32) * own_values[
        :, :, None, :
    ].astype(jnp.float32)
    return mixture.reshape(row_count, -1).astype(jnp.bfloat16)


def ffn_terms(
    rows_in, gate_blocks, up_blocks, gate_up_keep, gate_scale, up_scale, down_blocks, down_scale
):
    row_count = rows_in.shape[0]
    blocks = rows_in.reshape(row_count, -1, BLK)
    picked = blocks[:, gate_up_keep]
    gate_part = jnp.einsum(
        "rckd,ckdf->rckf", picked, gate_blocks, preferred_element_type=jnp.float32
    )
    up_part = jnp.einsum("rckd,ckdf->rckf", picked, up_blocks, preferred_element_type=jnp.float32)
    gate_sum = jnp.sum(gate_part * gate_scale[None, :, :, None], axis=2)
    up_sum = jnp.sum(up_part * up_scale[None, :, :, None], axis=2)
    hidden = (jax.nn.silu(gate_sum) * up_sum).astype(jnp.bfloat16)
    contrib = (
        jnp.einsum("rcf,ckfe->rcke", hidden, down_blocks, preferred_element_type=jnp.float32)
        * down_scale[None, :, :, None]
    )
    return contrib.reshape(row_count, -1, BLK)


def feed_forward(
    rows_in,
    gate_blocks,
    up_blocks,
    gate_up_keep,
    gate_scale,
    up_scale,
    down_blocks,
    down_keep,
    down_scale,
):
    row_count = rows_in.shape[0]
    contrib = ffn_terms(
        rows_in, gate_blocks, up_blocks, gate_up_keep, gate_scale, up_scale, down_blocks, down_scale
    )
    placed = jnp.zeros((row_count, rows_in.shape[1] // BLK, BLK), jnp.float32)
    placed = placed.at[:, down_keep.reshape(-1)].add(contrib)
    return placed.reshape(row_count, -1)


def per_device(
    branch_query,
    key_new,
    value_new,
    pool_pages,
    page_table,
    tail_length,
    parent_row,
    residual,
    norm_gain,
    gate_blocks,
    up_blocks,
    gate_up_keep,
    gate_scale,
    up_scale,
    down_blocks,
    down_keep,
    down_scale,
):
    row_count = branch_query.shape[0]
    tail_size = page_table.shape[1] * pool_pages.shape[2]
    own_tails = pool_pages[:, page_table].reshape(2, row_count, tail_size, pool_pages.shape[3])
    own_length = tail_length.astype(jnp.bfloat16)
    prior_tails, prior_length = shifted((own_tails, own_length), "wide", 1)
    both_tails = jnp.concatenate([prior_tails, own_tails], axis=1)
    both_length = jnp.concatenate([prior_length, own_length]).astype(jnp.float32)
    local_parent = parent_row - (lax.axis_index("wide") - 1) * row_count
    child_tails = both_tails[:, local_parent]
    child_length = both_length[local_parent]
    attention = attend(branch_query, key_new, value_new, child_tails, child_length)
    head_rows = lax.all_to_all(attention, "head", split_axis=0, concat_axis=1, tiled=True)
    middle = residual.astype(jnp.float32) + head_rows.astype(jnp.float32)
    normed = (
        middle * lax.rsqrt(jnp.mean(middle * middle, axis=-1, keepdims=True) + 1e-05) * norm_gain
    ).astype(jnp.bfloat16)
    gathered = lax.all_gather(normed, "wide", axis=0, tiled=True)
    ffn_share = lax.psum_scatter(
        feed_forward(
            gathered,
            gate_blocks,
            up_blocks,
            gate_up_keep,
            gate_scale,
            up_scale,
            down_blocks,
            down_keep,
            down_scale,
        ),
        "wide",
        scatter_dimension=0,
        tiled=True,
    )
    return (middle + ffn_share).astype(jnp.bfloat16)


def solution(mesh):
    placed = (
        P("wide", "head"),
        P("wide", "head"),
        P("wide", "head"),
        P(None, "wide", None, "head"),
        P("wide", None),
        P("wide"),
        P("wide"),
        P(("wide", "head"), None),
        P(),
        P("wide", None, None, None),
        P("wide", None, None, None),
        P("wide", None),
        P("wide", None),
        P("wide", None),
        P("wide", None, None, None),
        P("wide", None),
        P("wide", None),
    )
    return jax.shard_map(
        per_device, mesh=mesh, in_specs=placed, out_specs=P(("wide", "head"), None), check_vma=False
    )
```

profile of v0, /device:TPU:0, one launch (start us, length us, event | category | flops | bytes accessed | tf_op | source)
XLA Modules:
  0.0 1664.6 jit_solution(4971448282090236320)
XLA Ops:
  6.5 0.0 copy-start
  6.5 0.0 all-gather.3.cloned.1.call-start
  6.5 0.8 compare_select_fusion
  7.4 0.1 reshape.169
  7.5 0.7 copy-done
  8.2 0.0 copy-start.4
  8.2 2.0 gather_fusion.1
  10.2 3.1 copy.39
  13.3 2.6 collective-permute-start.1
  16.0 0.0 copy-done.10
  16.0 1.5 collective-permute-start
  17.5 0.0 copy-done.6
  17.5 0.0 copy-done.7
  17.5 0.0 copy-done.11
  17.5 0.0 copy-done.4
  17.6 0.1 fusion.21
  17.7 0.7 collective-permute-done
  18.4 0.1 maximum_convert_fusion
  18.5 0.6 gather_fusion
  19.1 0.1 iota_compare_fusion
  19.2 0.0 collective-permute-done.1
  19.2 4.5 pad_maximum_fusion
  23.7 2.9 gather_fusion.2
  26.6 1.2 fusion.33
  27.7 1.5 copy.40
  29.3 0.3 select_reduce_fusion
  29.6 0.2 bitcast_reduce_fusion
  29.8 0.5 copy.42
  30.4 0.4 fusion.5
  30.8 15.1 all_to_all.10
  45.9 0.0 copy-done.3
  46.0 0.2 multiply_reduce_fusion
  46.1 0.0 copy-done.5
  46.2 0.7 fusion.24
  46.9 0.0 all-gather.3.cloned.1.call-update
  46.9 0.2 all-reduce.3.cloned.1.call-start
  47.1 0.0 copy-done.12
  47.2 0.0 copy-done.13
  47.2 221.7 %all-gather.3.cloned.1.call-done = bf16[128,2,8192]{2,1,0:T(2,128)(2,1)} async-done(((bf16[1,2,8192]{2,1,0:T(2,128)(2,1)}), bf16[128,2,8192]{2,1,0:T(2,128)(2,1)}) %all-gather.3.cloned.1.call-update) | async-done | bytes 4194320 | tf_op jit(solution)/shard_map/all_gather | solution.py:128
  268.9 7.8 reshape.150
  276.7 6.9 copy.44
  283.6 3.2 gather_fusion.3
  286.8 0.0 copy-start.9
  286.8 0.0 copy-done.14
  286.8 0.0 copy-start.2
  286.8 0.0 copy-start.8
  286.8 2.1 fusion.1
  288.9 0.0 copy-done.15
  288.9 0.0 copy-done.9
  288.9 0.7 fusion.2
  289.6 0.0 copy-done.2
  289.6 0.0 copy-done.8
  289.7 2.7 fusion
  292.3 4.3 broadcast_in_dim.48
  296.6 10.2 scatter_fusion
  306.8 9.0 copy.45
  315.7 0.0 all-reduce.3.cloned.1.call-update
  315.8 0.6 copy-done.16
  316.4 0.6 dynamic-slice
  317.6 1331.2 %all-reduce.3.cloned.1.call-done = f32[256,8192]{0,1:T(8,128)} async-done(((f32[256,8192]{0,1:T(8,128)}), f32[256,8192]{0,1:T(8,128)}) %all-reduce.3.cloned.1.call-update) | async-done | bytes 8388624
  1648.8 5.4 constant_dynamic-slice_fusion
  1654.3 2.8 copy.46
  1657.1 0.7 add_convert_fusion
  1657.8 0.0 copy-done.1
  (26 shorter events, 0.2 us)
Async XLA Ops:
  6.5 1.6 copy-start
  6.5 262.4 %all-gather.3.cloned.1.call-start = ((), (), s32[]{:S(2)}) async-start(), calls=%async_computation.1 | async-start | bytes 4227072 | tf_op jit(solution)/shard_map/all_gather | solution.py:128
  8.1 7.8 copy-start.10
  8.1 9.3 copy-start.6
  8.1 9.3 copy-start.7
  8.1 9.4 copy-start.11
  8.2 9.4 copy-start.4
  13.3 5.8 collective-permute-start.1
  16.0 2.4 collective-permute-start
  27.7 18.2 %copy-start.3 = (bf16[2,8192]{1,0:T(2,128)(2,1)S(1)}, bf16[2,8192]{1,0:T(2,128)(2,1)}, u32[]{:S(2)}) copy-start(bf16[2,8192]{1,0:T(2,128)(2,1)} %param.24) | copy-start | bytes 98308
  27.7 18.4 %copy-start.5 = (f32[8192]{0:T(1024)S(1)}, f32[8192]{0:T(1024)}, u32[]{:S(2)}) copy-start(f32[8192]{0:T(1024)} %param.25) | copy-start | bytes 98308
  27.7 19.4 %copy-start.12 = (s32[1,32]{1,0:T(1,128)S(1)}, s32[1,32]{1,0:T(1,128)}, u32[]{:S(2)}) copy-start(s32[1,32]{1,0:T(1,128)} %param.28) | copy-start | bytes 388
  27.7 19.4 %copy-start.13 = (s32[1,32]{1,0:T(1,128)S(1)}, s32[1,32]{1,0:T(1,128)}, u32[]{:S(2)}) copy-start(s32[1,32]{1,0:T(1,128)} %param.32) | copy-start | bytes 388
  46.9 1601.9 %all-reduce.3.cloned.1.call-start = ((), (), s32[]{:S(2)}) async-start(), calls=%async_computation.2 | async-start | bytes 16777216
  283.6 3.2 copy-start.14
  283.6 5.3 copy-start.15
  286.8 2.1 copy-start.9
  286.8 2.9 copy-start.2
  286.8 2.8 copy-start.8
  315.7 0.7 copy-start.16
  1648.8 9.0 copy-start.1
Sparse Core Ops, SparseCore 0:
  47.0 221.8 all-gather.2
  315.9 1332.9 all-reduce.2
where the time goes:
time: 1670 us; the launch traced here: 1660 us
  waiting for transfers between devices  1550 us (93%)
  local copies, waits for them, and re-layouts  53.3 us (3%)
  other arithmetic  17.5 us (1%)
    unnamed x3, waiting for transfers between devices  1330 us
    all_gather x1, waiting for transfers between devices, per_device(): gathered = lax.all_gather(normed, 'wide', axis=0, tiled=True)  222 us
  transfers between devices with their start and end apart: 4, of which 3 were waited for; matrix products, arithmetic and copies ran while one was open for 0% of the time, Pallas kernels for 0%

commit v1 on v0

--- a/solution.py
+++ b/solution.py
@@ -125,7 +125,9 @@
     normed = (
         middle * lax.rsqrt(jnp.mean(middle * middle, axis=-1, keepdims=True) + 1e-05) * norm_gain
     ).astype(jnp.bfloat16)
-    gathered = lax.all_gather(normed, "wide", axis=0, tiled=True)
+    gathered = jnp.concatenate(
+        lax.all_to_all(jnp.stack([normed] * lax.axis_size("wide"), axis=0), "wide", 0, 0), axis=0
+    )
     ffn_share = lax.psum_scatter(
         feed_forward(
             gathered,

time: 1670 us -> 1570 us (0.940)
  waiting for transfers between devices: 1550 us -> 1420 us
  starting transfers between devices: 4.34 us -> 38.7 us
    all_gather x1 -> x0, waiting for transfers between devices: 222 us -> none  [per_device(): gathered = lax.all_gather(normed, 'wide', axis=0, tiled=True)]
    all_to_all x0 -> x1, waiting for transfers between devices: none -> 96.5 us  [per_device(): lax.all_to_all(jnp.stack([normed] * lax.axis_size('wide'), axis=0), 'wide...]
    all_to_all x0 -> x1, starting transfers between devices: none -> 34.4 us  [per_device(): lax.all_to_all(jnp.stack([normed] * lax.axis_size('wide'), axis=0), 'wide...]
    another operation x0 -> x3, local copies, waits for them, and re-layouts: none -> 20.9 us  [the longest x2 14.7 us: ffn_terms(): blocks = rows_in.reshape(row_count, -1, BLK)]
    unnamed x3 -> x2, waiting for transfers between devices: 1330 us -> 1330 us
where the time goes in v1:
time: 1570 us
  waiting for transfers between devices  1420 us (90%)
  local copies, waits for them, and re-layouts  59.5 us (4%)
  starting transfers between devices  38.7 us (2%)
  other arithmetic  17 us (1%)
    unnamed x2, waiting for transfers between devices  1330 us
    all_to_all x1, waiting for transfers between devices, per_device(): lax.all_to_all(jnp.stack([normed] * lax.axis_size('wide'), axis=0), 'wide...  96.5 us
    all_to_all x1, starting transfers between devices, per_device(): lax.all_to_all(jnp.stack([normed] * lax.axis_size('wide'), axis=0), 'wide...  34.4 us
  transfers between devices with their start and end apart: 4, of which 3 were waited for; matrix products, arithmetic and copies ran while one was open for 0% of the time, Pallas kernels for 0%

profile of v1, /device:TPU:0, one launch (start us, length us, event | category | flops | bytes accessed | tf_op | source)
XLA Modules:
  0.0 1574.0 jit_solution(11822017238873283817)
XLA Ops:
  6.5 0.0 copy-start
  6.5 0.8 compare_select_fusion
  7.4 0.1 reshape.167
  7.5 0.7 copy-done
  8.2 0.0 copy-start.4
  8.2 2.0 gather_fusion.1
  10.2 3.1 copy.60
  13.3 2.6 collective-permute-start.1
  15.9 0.0 copy-done.10
  16.0 1.5 collective-permute-start
  17.4 0.0 copy-done.6
  17.5 0.0 copy-done.7
  17.5 0.0 copy-done.11
  17.5 0.0 copy-done.4
  17.5 0.1 fusion.21
  17.7 0.7 collective-permute-done
  18.4 0.1 maximum_convert_fusion
  18.4 0.6 gather_fusion
  19.1 0.1 iota_compare_fusion
  19.2 0.0 collective-permute-done.1
  19.2 4.5 pad_maximum_fusion
  23.7 2.9 gather_fusion.2
  26.6 1.2 fusion.32
  27.7 1.5 copy.61
  29.2 0.3 select_reduce_fusion
  29.6 0.2 bitcast_reduce_fusion
  29.8 0.5 copy.63
  30.3 0.4 fusion.5
  30.8 15.1 all_to_all.15
  45.9 0.0 copy-done.3
  45.9 0.2 multiply_reduce_fusion
  46.1 0.0 copy-done.5
  46.1 0.1 multiply_convert_fusion
  46.2 6.2 stack.2
  52.4 34.4 %all-to-all-start.1 = ((bf16[128,2,8192]{2,1,0:T(2,128)(2,1)}), bf16[128,2,8192]{2,1,0:T(2,128)(2,1)}, u32[]{:S(2)}, u32[]{:S(2)}) async-start(bf16[128,2,8192]{2,1,0:T(2,128)(2,1)} %stack.2), calls=%async_computation.1 | async-start | bytes 8388608 | tf_op jit(solution)/shard_map/all_to_all | solution.py:129
  86.8 0.2 all-reduce.3.cloned.1.call-start
  87.0 0.0 copy-done.12
  87.0 0.0 copy-done.13
  87.1 96.5 %all-to-all-done.1 = bf16[128,2,8192]{2,1,0:T(2,128)(2,1)} async-done(((bf16[128,2,8192]{2,1,0:T(2,128)(2,1)}), bf16[128,2,8192]{2,1,0:T(2,128)(2,1)}, u32[]{:S(2)}, u32[]{:S(2)}) %all-to-all-start.1) | async-done | bytes 4194336 | tf_op jit(solution)/shard_map/all_to_all | solution.py:129
  183.6 7.9 reshape_reshape.3
  191.4 6.8 copy.65
  198.3 3.2 gather_fusion.3
  201.4 0.0 copy-start.9
  201.5 0.0 copy-done.14
  201.5 0.0 copy-start.2
  201.5 0.0 copy-start.8
  201.5 2.1 fusion.1
  203.6 0.0 copy-done.15
  203.6 0.0 copy-done.9
  203.6 0.7 fusion.2
  204.3 0.0 copy-done.2
  204.3 0.0 copy-done.8
  204.3 2.7 fusion
  207.0 4.3 broadcast_in_dim.48
  211.3 10.3 scatter_fusion
  221.5 9.0 copy.66
  230.5 0.0 all-reduce.3.cloned.1.call-update
  230.5 0.6 copy-done.16
  231.2 0.6 dynamic-slice
  232.4 1325.8 %all-reduce.3.cloned.1.call-done = f32[256,8192]{0,1:T(8,128)} async-done(((f32[256,8192]{0,1:T(8,128)}), f32[256,8192]{0,1:T(8,128)}) %all-reduce.3.cloned.1.call-update) | async-done | bytes 8388624
  1558.2 5.5 constant_dynamic-slice_fusion
  1563.6 2.8 copy.67
  1566.5 0.7 add_convert_fusion
  1567.1 0.0 copy-done.1
  (26 shorter events, 0.2 us)
Async XLA Ops:
  6.5 1.6 copy-start
  8.1 7.8 copy-start.10
  8.1 9.3 copy-start.6
  8.1 9.3 copy-start.7
  8.1 9.4 copy-start.11
  8.2 9.4 copy-start.4
  13.3 5.8 collective-permute-start.1
  16.0 2.4 collective-permute-start
  27.7 18.2 %copy-start.3 = (bf16[2,8192]{1,0:T(2,128)(2,1)S(1)}, bf16[2,8192]{1,0:T(2,128)(2,1)}, u32[]{:S(2)}) copy-start(bf16[2,8192]{1,0:T(2,128)(2,1)} %param.24) | copy-start | bytes 98308
  27.7 18.4 %copy-start.5 = (f32[8192]{0:T(1024)S(1)}, f32[8192]{0:T(1024)}, u32[]{:S(2)}) copy-start(f32[8192]{0:T(1024)} %param.25) | copy-start | bytes 98308
  52.4 34.7 %copy-start.12 = (s32[1,32]{1,0:T(1,128)S(1)}, s32[1,32]{1,0:T(1,128)}, u32[]{:S(2)}) copy-start(s32[1,32]{1,0:T(1,128)} %param.28) | copy-start | bytes 388
  52.4 34.7 %copy-start.13 = (s32[1,32]{1,0:T(1,128)S(1)}, s32[1,32]{1,0:T(1,128)}, u32[]{:S(2)}) copy-start(s32[1,32]{1,0:T(1,128)} %param.32) | copy-start | bytes 388
  52.4 131.2 %all-to-all-start.1 = ((bf16[128,2,8192]{2,1,0:T(2,128)(2,1)}), bf16[128,2,8192]{2,1,0:T(2,128)(2,1)}, u32[]{:S(2)}, u32[]{:S(2)}) async-start(bf16[128,2,8192]{2,1,0:T(2,128)(2,1)} %stack.2), calls=%async_computation.1 | async-start | bytes 8388608 | tf_op jit(solution)/shard_map/all_to_all | solution.py:129
  86.8 1471.4 %all-reduce.3.cloned.1.call-start = ((), (), s32[]{:S(2)}) async-start(), calls=%async_computation.2 | async-start | bytes 16777216
  198.3 3.2 copy-start.14
  198.3 5.3 copy-start.15
  201.4 2.1 copy-start.9
  201.5 2.9 copy-start.2
  201.5 2.9 copy-start.8
  230.5 0.7 copy-start.16
  1558.2 9.0 copy-start.1
Sparse Core Ops, SparseCore 0:
  230.6 1327.4 all-reduce.2
